TPU v7x, 256 devices: a whole 4x4x8 slice. The times are simulated.
256 devices in a mesh: date: 32 (over z, y_lo, core), strip: 8 (over x, y_hi).
Axes of the slice: x: 4, y: 4 (y_hi: 2, y_lo: 2; y = y_hi * 2 + y_lo), z: 8, core: 2. Of those that a mesh axis runs over, the one named last changes fastest.
Arguments:
- acquisitions: bfloat16 [64, 2, 2, 344, 2560], P('date', None, None, None, 'strip'), may hold values from -6 to 6
- shifts: int32 [2, 64, 2, 5, 40], P(None, 'date', None, None, 'strip'), may hold values from -8 to 8, as said below
- fractions: int32 [2, 64, 2, 5, 40], P(None, 'date', None, None, 'strip'), may hold values from 0 to 63
- ref_dates: int32 [2], replicated, may hold values from 0 to 63, as said below
Outputs:
- chip_corr: float32 [2, 64, 2, 5, 40], P(None, 'date', None, None, 'strip')
- coherence: float32 [2, 63, 2, 64, 128], P(None, None, None, 'date', 'strip')
Inputs may be any that keep to these rules, and one draw needn't show every extreme that they name: `shifts`: zero at every chip of date ref_dates[t] in tile t. `ref_dates`: the reference dates of consecutive tiles lie in different blocks of 2 dates.
All inputs are finite; a program needn't handle non-finite values.
Results may differ from a plain program's by a relative error of at most 0.0021.
Values may be sent and summed in bfloat16 or wider, within the bound.
No kernel may reach another device: no remote copies, remote signals or barrier semaphores. Data moves between devices by JAX's collectives and lax.ppermute only.
A program may use at most 64 MiB of HBM per device.

v0:
```python
import jax
import jax.numpy as jnp
from jax import lax
from jax.sharding import PartitionSpec as P

TILE_COUNT = 2
CHIP_SIZE = 64
TAP_COUNT = 8
SUBSTEPS = 64
LOOK_AZ = 5
LOOK_RG = 20
MARGIN = 12
epsilon = 1e-06


def padded_2(block, sides, width):
    for axis, dim in sides:
        count = lax.axis_size(axis)
        forward = [(i, i + 1) for i in range(count - 1)]
        backward = [(target, source) for source, target in forward]
        low = lax.ppermute(
            lax.slice_in_dim(block, block.shape[dim] - width, None, axis=dim), axis, forward
        )
        high = lax.ppermute(lax.slice_in_dim(block, 0, width, axis=dim), axis, backward)
        block = jnp.concatenate([low, block, high], axis=dim)
    return block


def spread(value, axis, source):
    kept = jnp.where(lax.axis_index(axis) == source, value, 0).astype(value.dtype)
    return lax.psum(kept, axis)


def sinc_matrix(shift_part, fraction_part):
    window_size = CHIP_SIZE + 2 * MARGIN
    offset = fraction_part.astype(jnp.float32) / SUBSTEPS
    tap_axis = jnp.arange(TAP_COUNT).astype(jnp.float32)
    distance = tap_axis - (TAP_COUNT // 2 - 1) - offset[..., None]
    weights = jnp.sinc(distance) * (0.5 + 0.5 * jnp.cos(jnp.pi * distance / (TAP_COUNT // 2)))
    weights = weights / jnp.sum(weights, axis=-1, keepdims=True)
    out_rows = jnp.arange(CHIP_SIZE, dtype=jnp.int32)[:, None]
    in_rows = jnp.arange(window_size, dtype=jnp.int32)[None, :]
    matrix = jnp.zeros(shift_part.shape + (CHIP_SIZE, window_size), jnp.float32)
    for tap_index in range(TAP_COUNT):
        target = out_rows + shift_part[..., None, None] + (tap_index - TAP_COUNT // 2 + 1 + MARGIN)
        matrix = matrix + jnp.where(
            in_rows == target, weights[..., tap_index][..., None, None], 0.0
        )
    return matrix.astype(jnp.bfloat16)


def correlate(reference_tiles, resampled):
    chips_az = resampled.shape[-2] // CHIP_SIZE
    chips_rg = resampled.shape[-1] // CHIP_SIZE

    def as_chips(values):
        return values.astype(jnp.float32).reshape(
            values.shape[:-2] + (chips_az, CHIP_SIZE, chips_rg, CHIP_SIZE)
        )

    ref_chips = as_chips(reference_tiles)
    sec_chips = as_chips(resampled)
    ref_real = ref_chips[..., 0, :, :, :, :]
    ref_imag = ref_chips[..., 1, :, :, :, :]
    sec_real = sec_chips[..., 0, :, :, :, :]
    sec_imag = sec_chips[..., 1, :, :, :, :]
    cross_real = jnp.sum(ref_real * sec_real + ref_imag * sec_imag, axis=(-3, -1))
    cross_imag = jnp.sum(ref_imag * sec_real - ref_real * sec_imag, axis=(-3, -1))
    ref_power = jnp.sum(ref_real * ref_real + ref_imag * ref_imag, axis=(-3, -1))
    sec_power = jnp.sum(sec_real * sec_real + sec_imag * sec_imag, axis=(-3, -1))
    denominator = jnp.sqrt((ref_power + epsilon) * (sec_power + epsilon))
    return jnp.stack([cross_real / denominator, cross_imag / denominator])


def multilook_pairs(series):
    values = series.astype(jnp.float32)
    earlier = values[:-1]
    second = values[1:]
    early_real = earlier[:, :, 0]
    early_imag = earlier[:, :, 1]
    later_real = second[:, :, 0]
    later_imag = second[:, :, 1]
    cross_real = early_real * later_real + early_imag * later_imag
    cross_imag = early_imag * later_real - early_real * later_imag
    power_early = early_real * early_real + early_imag * early_imag
    power_later = later_real * later_real + later_imag * later_imag

    def box_sum(quantity):
        blocked = quantity.reshape(
            quantity.shape[:2]
            + (quantity.shape[2] // LOOK_AZ, LOOK_AZ, quantity.shape[3] // LOOK_RG, LOOK_RG)
        )
        return jnp.sum(blocked, axis=(3, 5))

    denominator = jnp.sqrt((box_sum(power_early) + epsilon) * (box_sum(power_later) + epsilon))
    return jnp.stack([box_sum(cross_real) / denominator, box_sum(cross_imag) / denominator])


def resample(padded, shift_part, fraction_part):
    window_size = CHIP_SIZE + 2 * MARGIN
    chips_az = shift_part.shape[3]
    chips_rg = shift_part.shape[4]
    pieces = [
        padded[
            :,
            :,
            :,
            chip_row * CHIP_SIZE : chip_row * CHIP_SIZE + window_size,
            chip_col * CHIP_SIZE : chip_col * CHIP_SIZE + window_size,
        ]
        for chip_row in range(chips_az)
        for chip_col in range(chips_rg)
    ]
    windows = jnp.stack(pieces, axis=3).reshape(
        padded.shape[:3] + (chips_az, chips_rg, window_size, window_size)
    )
    azimuth = sinc_matrix(shift_part[0], fraction_part[0])
    across = sinc_matrix(shift_part[1], fraction_part[1])
    partial_rows = jnp.einsum(
        "dtariw,dtcarwv->dtcariv", azimuth, windows, preferred_element_type=jnp.float32
    ).astype(jnp.bfloat16)
    chips_out = jnp.einsum(
        "dtcariv,dtarjv->dtcarij", partial_rows, across, preferred_element_type=jnp.float32
    ).astype(jnp.bfloat16)
    return chips_out.transpose(0, 1, 2, 3, 5, 4, 6).reshape(
        padded.shape[:3] + (chips_az * CHIP_SIZE, chips_rg * CHIP_SIZE)
    )


def per_device(acquisitions, shifts, fractions, ref_dates):
    dates_local = acquisitions.shape[0]
    tile_rows = acquisitions.shape[3] - 2 * MARGIN
    padded = padded_2(acquisitions, (("strip", 4),), MARGIN)
    owners = ref_dates // dates_local
    slots = ref_dates % dates_local
    candidates = [
        lax.dynamic_index_in_dim(acquisitions[:, tile_index], slots[tile_index], 0, keepdims=False)[
            :, MARGIN : MARGIN + tile_rows, :
        ]
        for tile_index in range(TILE_COUNT)
    ]
    reference_tiles = jnp.stack(
        [
            spread(candidates[tile_index], "date", owners[tile_index])
            for tile_index in range(TILE_COUNT)
        ]
    )
    resampled = resample(padded, shifts, fractions)
    chip_corr = correlate(reference_tiles, resampled)
    coherence = multilook_pairs(
        lax.all_to_all(resampled, "date", split_axis=3, concat_axis=0, tiled=True)
    )
    return (chip_corr, coherence)


def solution(mesh):
    return jax.shard_map(
        per_device,
        mesh=mesh,
        in_specs=(
            P("date", None, None, None, "strip"),
            P(None, "date", None, None, "strip"),
            P(None, "date", None, None, "strip"),
            P(),
        ),
        out_specs=(P(None, "date", None, None, "strip"), P(None, None, None, "date", "strip")),
        check_vma=False,
    )
```

profile of v0, /device:TPU:1, one launch (start us, length us, event | category | flops | bytes accessed | tf_op | source)
XLA Modules:
  0.0 462.1 jit_solution(9222938451931565228)
XLA Ops:
  10.2 6.3 %collective-permute-start = (bf16[2,2,2,344,12]{3,4,2,1,0:T(8,128)(2,1)}, bf16[2,2,2,344,12]{3,4,2,1,0:T(8,128)(2,1)S(1)}, u32[]{:S(2)}, u32[]{:S(2)}) collective-permute-start(bf16[2,2,2,344,12]{3,4,2,1,0:T(8,128)(2,1)} %get-tuple-element.23), channel_id=1, source_target_pairs={{0,1},{1,2},{2,3},{3,4},{4,5},{5,6},{6,7},{8,9},{9,10},{10,11},{11... | collective-permute-start | bytes 198152 | tf_op jit(solution)/shard_map/ppermute | solution.py:21
  25.9 3.2 fusion.114
  29.1 3.1 broadcast_divide_fusion.1
  71.7 7.4 %copy.137 = bf16[2,2,2,25,88,88]{5,4,2,3,1,0:T(8,128)(2,1)} copy(bf16[2,2,2,25,88,88]{4,5,2,1,0,3:T(8,128)(2,1)} %fusion.62) | data formatting | bytes 6195200 | tf_op jit(solution)/shard_map/stack | solution.py:114
  79.4 13.2 %fusion.4.clone.5 = bf16[2,2,2,5,5,64,88]{6,5,2,4,3,1,0:T(8,128)(2,1)S(1)} fusion(bf16[2,2,2,5,5,88,88]{6,5,2,4,3,1,0:T(8,128)(2,1)} %bitcast.220, f32[2,2,5,5]{3,2,1,0:T(8,128)S(1)} %copy-done.26, s32[2,2,5,5,64]{4,3,2,1,0:T(8,128)S(1)} %copy-done.11, f32[2,2,5,5]{3,2,1,0:T(8,128)S(1)} %copy-done.28, ...), kind=kOutput, calls=%fused_computation.3.clone.clone.clone.clone.clone.2 | convolution fusion | flops 212889600 | bytes 5558400 | tf_op jit(solution)/shard_map/dtariw,dtcarwv->dtcariv/dot_general | solution.py:119
  92.7 13.8 %fusion.122 = (f32[2,2,2,5,64,5,64]{4,6,2,5,3,1,0:T(8,128)}, bf16[2,2,2,5,64,5,64]{4,6,2,5,3,1,0:T(8,128)(2,1)}) fusion(f32[2,2,5,5]{3,2,1,0:T(8,128)S(1)} %copy-done.27, s32[2,2,5,5,64]{4,3,2,1,0:T(8,128)S(1)} %copy-done.8, f32[2,2,5,5]{3,2,1,0:T(8,128)S(1)} %copy-done.25, s32[2,2,5,5,64]{4,3,2,1,0:T(8,128)S(1)} %copy-done.7, ...), kind=kOutput, calls=%fused_computation.226 | convolution fusion | flops 159334400 | bytes 7376000 | tf_op jit(solution)/shard_map/dtcariv,dtarjv->dtcarij/dot_general | solution.py:122
  106.5 7.8 %copy.165 = bf16[2,2,2,5,64,5,64]{6,5,2,1,0,4,3:T(8,128)(2,1)} copy(bf16[2,2,2,5,64,5,64]{4,6,2,5,3,1,0:T(8,128)(2,1)} %get-tuple-element.73) | data formatting | bytes 3276800 | tf_op jit(solution)/shard_map/reshape | solution.py:125
  114.3 8.2 %reshape.249 = bf16[2,2,2,320,320]{4,2,1,0,3:T(2,128)(2,1)} reshape(bf16[2,2,2,5,64,5,64]{6,5,2,1,0,4,3:T(8,128)(2,1)} %copy.165) | data formatting | bytes 3276800 | tf_op jit(solution)/shard_map/reshape | solution.py:125
  122.5 11.0 %all-to-all-start = ((bf16[2,2,2,320,320]{4,2,1,0,3:T(2,128)(2,1)}), bf16[2,2,2,320,320]{4,2,1,0,3:T(2,128)(2,1)S(1)}, u32[]{:S(2)}, u32[]{:S(2)}) async-start(bf16[2,2,2,320,320]{4,2,1,0,3:T(2,128)(2,1)} %reshape.249), calls=%async_computation | async-start | bytes 3932160 | tf_op jit(solution)/shard_map/all_to_all | solution.py:151
  137.7 245.5 %all-reduce.3.cloned.1.call-done = (bf16[1,2,5,64,5,64]{5,4,3,2,1,0:T(8,128)(2,1)}, bf16[1,2,5,64,5,64]{5,4,3,2,1,0:T(8,128)(2,1)}) async-done(((bf16[1,2,5,64,5,64]{5,4,3,2,1,0:T(8,128)(2,1)}, bf16[1,2,5,64,5,64]{5,4,3,2,1,0:T(8,128)(2,1)}), (bf16[1,2,5,64,5,64]{5,4,3,2,1,0:T(8,128)(2,1)}, bf16[1,2,5,64,5,64]{5,4,3,2,1,0:T(8,128)(2,1)})) %all-reduce.3.cloned.1.call-update) | async-done | bytes 819216 | tf_op jit(solution)/shard_map/psum | solution.py:31
  386.5 2.8 slice_bitcast_fusion.3
  389.3 2.9 copy.127
  392.2 2.9 copy.148
  395.1 4.9 %add_reduce_fusion.1 = (f32[2,2,5,5]{3,2,1,0:T(8,128)S(1)}, f32[2,2,5,5]{3,2,1,0:T(8,128)S(1)}, f32[2,2,5,5]{3,2,1,0:T(8,128)S(1)}) fusion(f32[2,2,2,5,64,5,64]{4,6,2,5,3,1,0:T(8,128)} %get-tuple-element.72, f32[2,5,64,5,64]{2,4,3,1,0:T(8,128)} %copy.148, f32[2,5,64,5,64]{2,4,3,1,0:T(8,128)} %copy.127), kind=kLoop, calls=%fused_computation.6 | loop fusion | flops 4914900 | bytes 4916400 | tf_op jit(solution)/shard_map/reduce_sum | solution.py:67
  400.9 3.0 copy.156
  405.3 9.2 %multiply_add_fusion.2 = (f32[63,2,1,10,320]{4,2,3,1,0:T(1,128)}, f32[63,2,1,10,320]{4,2,3,1,0:T(1,128)}, f32[63,2,1,10,320]{4,2,3,1,0:T(1,128)}, f32[63,2,1,10,320]{4,2,3,1,0:T(1,128)S(1)}) fusion(f32[64,2,2,10,320]{4,2,3,1,0:T(2,128)S(1)} %bitcast.214), kind=kLoop, calls=%fused_computation.35 | loop fusion | flops 4838400 | bytes 12902400 | tf_op jit(solution)/shard_map/add | solution.py:83
  414.5 7.4 %copy.158 = f32[63,2,1,10,320]{0,1,4,3,2:T(2,128)} copy(f32[63,2,1,10,320]{4,2,3,1,0:T(1,128)} %get-tuple-element.16) | data formatting | bytes 3225600 | tf_op jit(solution)/shard_map/add | solution.py:83
  421.9 7.4 %copy.159 = f32[63,2,1,10,320]{0,1,4,3,2:T(2,128)} copy(f32[63,2,1,10,320]{4,2,3,1,0:T(1,128)} %get-tuple-element.17) | data formatting | bytes 3225600 | tf_op jit(solution)/shard_map/add | solution.py:85
  429.3 3.2 reduce_sum.102
  432.5 3.2 reduce_sum.103
  435.7 7.4 %copy.160 = f32[63,2,1,10,320]{0,1,4,3,2:T(2,128)} copy(f32[63,2,1,10,320]{4,2,3,1,0:T(1,128)} %get-tuple-element.18) | data formatting | bytes 3225600 | tf_op jit(solution)/shard_map/add | solution.py:86
  443.1 3.2 reduce_sum.104
  446.3 4.9 %copy.161 = f32[63,2,1,10,320]{0,1,4,3,2:T(2,128)} copy(f32[63,2,1,10,320]{4,2,3,1,0:T(1,128)S(1)} %get-tuple-element.19) | data formatting | bytes 3225600 | tf_op jit(solution)/shard_map/sub | solution.py:84
  451.3 3.2 reduce_sum.105
  (150 shorter events, 57.2 us)
Async XLA Ops:
  7.2 15.9 %copy-start = (bf16[2,2,2,344,320]{3,4,2,1,0:T(8,128)(2,1)S(1)}, bf16[2,2,2,344,320]{3,4,2,1,0:T(8,128)(2,1)}, u32[]{:S(2)}) copy-start(bf16[2,2,2,344,320]{3,4,2,1,0:T(8,128)(2,1)} %param.5) | copy-start | bytes 5283844
  9.0 39.9 %collective-permute-start.1 = (bf16[2,2,2,344,12]{3,4,2,1,0:T(8,128)(2,1)}, bf16[2,2,2,344,12]{3,4,2,1,0:T(8,128)(2,1)}, u32[]{:S(2)}, u32[]{:S(2)}) collective-permute-start(bf16[2,2,2,344,12]{3,4,2,1,0:T(8,128)(2,1)} %get-tuple-element.22), channel_id=1, source_target_pairs={{1,0},{2,1},{3,2},{4,3},{5,4},{6,5},{7,6},{9,8},{10,9},{11,10},{12... | collective-permute-start | bytes 198152 | tf_op jit(solution)/shard_map/ppermute | solution.py:24
  10.2 35.7 %collective-permute-start = (bf16[2,2,2,344,12]{3,4,2,1,0:T(8,128)(2,1)}, bf16[2,2,2,344,12]{3,4,2,1,0:T(8,128)(2,1)S(1)}, u32[]{:S(2)}, u32[]{:S(2)}) collective-permute-start(bf16[2,2,2,344,12]{3,4,2,1,0:T(8,128)(2,1)} %get-tuple-element.23), channel_id=1, source_target_pairs={{0,1},{1,2},{2,3},{3,4},{4,5},{5,6},{6,7},{8,9},{9,10},{10,11},{11... | collective-permute-start | bytes 198152 | tf_op jit(solution)/shard_map/ppermute | solution.py:21
  71.6 7.5 %copy-start.14 = (s32[2,2,5,5,64]{4,3,2,1,0:T(8,128)S(1)}, s32[2,2,5,5,64]{4,3,2,1,0:T(8,128)}, u32[]{:S(2)}) copy-start(s32[2,2,5,5,64]{4,3,2,1,0:T(8,128)} %get-tuple-element.60) | copy-start | bytes 76804
  71.6 7.5 %copy-start.15 = (s32[2,2,5,5,64]{4,3,2,1,0:T(8,128)S(1)}, s32[2,2,5,5,64]{4,3,2,1,0:T(8,128)}, u32[]{:S(2)}) copy-start(s32[2,2,5,5,64]{4,3,2,1,0:T(8,128)} %get-tuple-element.61) | copy-start | bytes 76804
  71.6 7.5 %copy-start.16 = (s32[2,2,5,5,64]{4,3,2,1,0:T(8,128)S(1)}, s32[2,2,5,5,64]{4,3,2,1,0:T(8,128)}, u32[]{:S(2)}) copy-start(s32[2,2,5,5,64]{4,3,2,1,0:T(8,128)} %get-tuple-element.62) | copy-start | bytes 76804
  79.2 13.4 %copy-start.2 = (s32[2,2,5,5,64]{4,3,2,1,0:T(8,128)S(1)}, s32[2,2,5,5,64]{4,3,2,1,0:T(8,128)}, u32[]{:S(2)}) copy-start(s32[2,2,5,5,64]{4,3,2,1,0:T(8,128)} %get-tuple-element.84) | copy-start | bytes 76804
  79.2 13.4 %copy-start.3 = (s32[2,2,5,5,64]{4,3,2,1,0:T(8,128)S(1)}, s32[2,2,5,5,64]{4,3,2,1,0:T(8,128)}, u32[]{:S(2)}) copy-start(s32[2,2,5,5,64]{4,3,2,1,0:T(8,128)} %get-tuple-element.85) | copy-start | bytes 76804
  79.2 13.4 %copy-start.4 = (s32[2,2,5,5,64]{4,3,2,1,0:T(8,128)S(1)}, s32[2,2,5,5,64]{4,3,2,1,0:T(8,128)}, u32[]{:S(2)}) copy-start(s32[2,2,5,5,64]{4,3,2,1,0:T(8,128)} %get-tuple-element.86) | copy-start | bytes 76804
  79.2 13.4 %copy-start.5 = (s32[2,2,5,5,64]{4,3,2,1,0:T(8,128)S(1)}, s32[2,2,5,5,64]{4,3,2,1,0:T(8,128)}, u32[]{:S(2)}) copy-start(s32[2,2,5,5,64]{4,3,2,1,0:T(8,128)} %get-tuple-element.87) | copy-start | bytes 76804
  79.3 13.4 %copy-start.6 = (s32[2,2,5,5,64]{4,3,2,1,0:T(8,128)S(1)}, s32[2,2,5,5,64]{4,3,2,1,0:T(8,128)}, u32[]{:S(2)}) copy-start(s32[2,2,5,5,64]{4,3,2,1,0:T(8,128)} %get-tuple-element.88) | copy-start | bytes 76804
  79.3 13.4 %copy-start.7 = (s32[2,2,5,5,64]{4,3,2,1,0:T(8,128)S(1)}, s32[2,2,5,5,64]{4,3,2,1,0:T(8,128)}, u32[]{:S(2)}) copy-start(s32[2,2,5,5,64]{4,3,2,1,0:T(8,128)} %get-tuple-element.89) | copy-start | bytes 76804
  79.3 13.4 %copy-start.8 = (s32[2,2,5,5,64]{4,3,2,1,0:T(8,128)S(1)}, s32[2,2,5,5,64]{4,3,2,1,0:T(8,128)}, u32[]{:S(2)}) copy-start(s32[2,2,5,5,64]{4,3,2,1,0:T(8,128)} %get-tuple-element.90) | copy-start | bytes 76804
  79.3 13.4 %copy-start.9 = (s32[2,2,5,5,64]{4,3,2,1,0:T(8,128)S(1)}, s32[2,2,5,5,64]{4,3,2,1,0:T(8,128)}, u32[]{:S(2)}) copy-start(s32[2,2,5,5,64]{4,3,2,1,0:T(8,128)} %get-tuple-element.91) | copy-start | bytes 76804
  79.3 13.4 %copy-start.20 = (f32[2,2,5,5]{3,2,1,0:T(8,128)S(1)}, f32[2,2,5,5]{3,2,1,0:T(8,128)}, u32[]{:S(2)}) copy-start(f32[2,2,5,5]{3,2,1,0:T(8,128)} %copy.131) | copy-start | bytes 1204
  79.3 13.4 %copy-start.21 = (f32[2,2,5,5]{3,2,1,0:T(8,128)S(1)}, f32[2,2,5,5]{3,2,1,0:T(8,128)}, u32[]{:S(2)}) copy-start(f32[2,2,5,5]{3,2,1,0:T(8,128)} %copy.132) | copy-start | bytes 1204
  79.3 13.4 %copy-start.22 = (f32[2,2,5,5]{3,2,1,0:T(8,128)S(1)}, f32[2,2,5,5]{3,2,1,0:T(8,128)}, u32[]{:S(2)}) copy-start(f32[2,2,5,5]{3,2,1,0:T(8,128)} %copy.133) | copy-start | bytes 1204
  79.3 13.4 %copy-start.23 = (f32[2,2,5,5]{3,2,1,0:T(8,128)S(1)}, f32[2,2,5,5]{3,2,1,0:T(8,128)}, u32[]{:S(2)}) copy-start(f32[2,2,5,5]{3,2,1,0:T(8,128)} %copy.134) | copy-start | bytes 1204
  79.3 13.4 %copy-start.25 = (f32[2,2,5,5]{3,2,1,0:T(8,128)S(1)}, f32[2,2,5,5]{3,2,1,0:T(8,128)}, u32[]{:S(2)}) copy-start(f32[2,2,5,5]{3,2,1,0:T(8,128)} %copy.135) | copy-start | bytes 1204
  79.3 13.4 %copy-start.27 = (f32[2,2,5,5]{3,2,1,0:T(8,128)S(1)}, f32[2,2,5,5]{3,2,1,0:T(8,128)}, u32[]{:S(2)}) copy-start(f32[2,2,5,5]{3,2,1,0:T(8,128)} %copy.136) | copy-start | bytes 1204
  79.4 13.4 %copy-start.30 = (f32[2,2,5,5]{3,2,1,0:T(8,128)S(1)}, f32[2,2,5,5]{3,2,1,0:T(8,128)}, u32[]{:S(2)}) copy-start(f32[2,2,5,5]{3,2,1,0:T(8,128)} %copy.129) | copy-start | bytes 1204
  122.5 11.3 %copy-start.1 = (bf16[2,344,320]{1,2,0:T(8,128)(2,1)S(1)}, bf16[2,344,320]{1,2,0:T(8,128)(2,1)}, u32[]{:S(2)}) copy-start(bf16[2,344,320]{1,2,0:T(8,128)(2,1)} %dynamic-slice_bitcast_fusion) | copy-start | bytes 1320964
  122.5 278.2 %all-to-all-start = ((bf16[2,2,2,320,320]{4,2,1,0,3:T(2,128)(2,1)}), bf16[2,2,2,320,320]{4,2,1,0,3:T(2,128)(2,1)S(1)}, u32[]{:S(2)}, u32[]{:S(2)}) async-start(bf16[2,2,2,320,320]{4,2,1,0,3:T(2,128)(2,1)} %reshape.249), calls=%async_computation | async-start | bytes 3932160 | tf_op jit(solution)/shard_map/all_to_all | solution.py:151
  133.5 249.7 %all-reduce.3.cloned.1.call-start = ((), (), s32[]{:S(2)}) async-start(), calls=%async_computation.1 | async-start | bytes 5242880 | tf_op jit(solution)/shard_map/psum | solution.py:31
  (15 other events, 108.8 us)
Sparse Core Ops, SparseCore 0:
  137.8 245.3 all-reduce.2
where the time goes:
time: 464 us; the launch traced here: 462 us
  waiting for transfers between devices  245 us (53%)
  local copies, waits for them, and re-layouts  107 us (23%)
  other arithmetic  43.7 us (9%)
  matrix products  27 us (6%)
  between operations  19.7 us (4%)
  starting transfers between devices  18.8 us (4%)
    psum x1, waiting for transfers between devices, spread(): return lax.psum(kept, axis)  245 us
    unnamed x91, local copies, waits for them, and re-layouts  20.8 us
    reshape x2, local copies, waits for them, and re-layouts, resample(): chips_out.transpose(0, 1, 2, 3, 5, 4, 6)  15.9 us
    dot_general x1, matrix products, resample(): jnp.einsum('dtcariv,dtarjv->dtcarij', partial_rows, across, preferred_ele...  13.8 us
    dot_general x1, matrix products, resample(): jnp.einsum('dtariw,dtcarwv->dtcariv', azimuth, windows, preferred_element...  13.2 us
    reduce_sum x4, other arithmetic, box_sum(): return jnp.sum(blocked, axis=(3, 5))  12.9 us
    all_to_all x1, starting transfers between devices, per_device(): lax.all_to_all(resampled, 'date', split_axis=3, concat_axis=0, tiled=True)  11 us
  transfers between devices with their start and end apart: 4, of which 1 were waited for; matrix products, arithmetic and copies ran while one was open for 10% of the time, Pallas kernels for 0%

commit v1 on v0

--- a/solution.py
+++ b/solution.py
@@ -28,7 +28,7 @@
 
 def spread(value, axis, source):
     kept = jnp.where(lax.axis_index(axis) == source, value, 0).astype(value.dtype)
-    return lax.psum(kept, axis)
+    return jnp.sum(lax.all_gather(kept, axis), axis=0)
 
 
 def sinc_matrix(shift_part, fraction_part):

time: 464 us -> 274 us (0.59)
  waiting for transfers between devices: 245 us -> 4.04 us
  blocking collectives: 0 us -> 68.7 us
  local copies, waits for them, and re-layouts: 107 us -> 86 us
  other arithmetic: 43.7 us -> 59.6 us
  starting transfers between devices: 18.8 us -> 7.65 us
    psum x1 -> x0, waiting for transfers between devices: 245 us -> none  [spread(): return lax.psum(kept, axis)]
    all_to_all x0 -> x1, blocking collectives: none -> 68.7 us  [per_device(): lax.all_to_all(resampled, 'date', split_axis=3, concat_axis=0, tiled=True)]
    reduce_sum x0 -> x2, other arithmetic: none -> 17.4 us  [spread(): return jnp.sum(lax.all_gather(kept, axis), axis=0)]
    all_to_all x1 -> x0, starting transfers between devices: 11 us -> none  [per_device(): lax.all_to_all(resampled, 'date', split_axis=3, concat_axis=0, tiled=True)]
    broadcast_in_dim x17, local copies, waits for them, and re-layouts: 9.06 us -> 0.08 us  [sinc_matrix(): jnp.where(in_rows == target, weights[..., tap_index][..., None, None], 0.0)]
    unnamed x91 -> x27, local copies, waits for them, and re-layouts: 20.8 us -> 15.5 us
  transfers between devices with their start and end apart: 4 -> 4, of which waited for: 1 -> 1; matrix products, arithmetic and copies ran while one was open for 10% -> 51% of each run, Pallas kernels for 0% -> 0%
where the time goes in v1:
time: 274 us; the launch traced here: 273 us
  local copies, waits for them, and re-layouts  86 us (31%)
  blocking collectives  68.7 us (25%)
  other arithmetic  59.6 us (22%)
  matrix products  26.8 us (10%)
  between operations  19.7 us (7%)
  starting transfers between devices  7.65 us (3%)
  waiting for transfers between devices  4.04 us (1%)
    all_to_all x1, blocking collectives, per_device(): lax.all_to_all(resampled, 'date', split_axis=3, concat_axis=0, tiled=True)  68.7 us
    reduce_sum x2, other arithmetic, spread(): return jnp.sum(lax.all_gather(kept, axis), axis=0)  17.4 us
    unnamed x27, local copies, waits for them, and re-layouts  15.5 us
    reshape x2, local copies, waits for them, and re-layouts, resample(): chips_out.transpose(0, 1, 2, 3, 5, 4, 6)  15.2 us
    dot_general x1, matrix products, resample(): jnp.einsum('dtcariv,dtarjv->dtcarij', partial_rows, across, preferred_ele...  13.8 us
    reduce_sum x4, other arithmetic, box_sum(): return jnp.sum(blocked, axis=(3, 5))  13.1 us
    dot_general x1, matrix products, resample(): jnp.einsum('dtariw,dtcarwv->dtcariv', azimuth, windows, preferred_element...  13 us
    add x1, other arithmetic, multilook_pairs(): cross_real = early_real * later_real + early_imag * later_imag  9.16 us
  transfers between devices with their start and end apart: 4, of which 1 were waited for; matrix products, arithmetic and copies ran while one was open for 51% of the time, Pallas kernels for 0%

profile of v1, /device:TPU:1, one launch (start us, length us, event | category | flops | bytes accessed | tf_op | source)
XLA Modules:
  0.0 272.5 jit_solution(8703010946431363026)
XLA Ops:
  23.5 6.3 %collective-permute-start = (bf16[2,2,2,344,12]{3,4,2,1,0:T(8,128)(2,1)S(1)}, bf16[2,2,2,344,12]{3,4,2,1,0:T(8,128)(2,1)S(1)}, u32[]{:S(2)}, u32[]{:S(2)}) collective-permute-start(bf16[2,2,2,344,12]{3,4,2,1,0:T(8,128)(2,1)S(1)} %get-tuple-element.21), channel_id=1, source_target_pairs={{0,1},{1,2},{2,3},{3,4},{4,5},{5,6},{6,7},{8,9},{9,10},{10,11},{11... | collective-permute-start | bytes 198152 | tf_op jit(solution)/shard_map/ppermute | solution.py:21
  29.9 3.2 %fusion.114 = (f32[2,2,5,5]{3,1,2,0:T(2,128)S(1)}, f32[2,2,5,5]{3,1,2,0:T(2,128)S(1)}) fusion(f32[2,2,5,5]{3,1,2,0:T(2,128)S(1)} %get-tuple-element.45, f32[8]{0:T(128)S(1)} %convert_add_fusion, f32[2,2,5,5]{3,1,2,0:T(2,128)S(1)} %get-tuple-element.44), kind=kLoop, calls=%fused_computation.182 | loop fusion | flops 62200 | bytes 1632 | tf_op jit(solution)/shard_map/reduce_sum | solution.py:40
  33.0 3.1 %broadcast_divide_fusion.1 = (f32[2,2,5,5,8]{3,1,2,0,4:T(2,128)S(1)}, f32[2,2,5,5,8]{3,1,2,0,4:T(2,128)S(1)}) fusion(f32[2,2,5,5]{3,1,2,0:T(2,128)S(1)} %get-tuple-element.10, f32[2,2,5,5]{3,1,2,0:T(2,128)S(1)} %get-tuple-element.45, f32[8]{0:T(128)S(1)} %convert_add_fusion, f32[2,2,5,5]{3,1,2,0:T(2,128)S(1)} %get-tuple-element.11, ...), kind=kLoop, calls=%fused_computation.180 | loop fusion | flops 62400 | bytes 8032 | tf_op jit(solution)/shard_map/div | solution.py:40
  56.2 7.2 %copy.113 = bf16[2,2,2,25,88,88]{5,4,2,3,1,0:T(8,128)(2,1)} copy(bf16[2,2,2,25,88,88]{4,5,2,1,0,3:T(8,128)(2,1)} %fusion.62) | data formatting | bytes 6195200 | tf_op jit(solution)/shard_map/stack | solution.py:114
  63.4 13.0 %fusion.4.clone.5 = bf16[2,2,2,5,5,64,88]{6,5,2,4,3,1,0:T(8,128)(2,1)S(1)} fusion(bf16[2,2,2,5,5,88,88]{6,5,2,4,3,1,0:T(8,128)(2,1)} %bitcast.222, f32[2,2,5,5]{3,2,1,0:T(8,128)S(1)} %copy.122, s32[2,2,5,5,64]{4,3,2,1,0:T(8,128)S(1)} %get-tuple-element.55, f32[2,2,5,5]{3,2,1,0:T(8,128)S(1)} %copy.121, ...), kind=kOutput, calls=%fused_computation.3.clone.clone.clone.clone.clone.2 | convolution fusion | flops 212889600 | bytes 5558400 | tf_op jit(solution)/shard_map/dtariw,dtcarwv->dtcariv/dot_general | solution.py:119
  76.4 13.8 %fusion.122 = (f32[2,2,2,5,64,5,64]{4,6,2,5,3,1,0:T(8,128)}, bf16[2,2,2,5,64,5,64]{4,6,2,5,3,1,0:T(8,128)(2,1)}) fusion(f32[2,2,5,5]{3,2,1,0:T(8,128)S(1)} %copy.112, s32[2,2,5,5,64]{4,3,2,1,0:T(8,128)S(1)} %get-tuple-element.88, f32[2,2,5,5]{3,2,1,0:T(8,128)S(1)} %copy.111, s32[2,2,5,5,64]{4,3,2,1,0:T(8,128)S(1)} %get-tuple-element.87, ...), kind=kOutput, calls=%fused_computation.226 | convolution fusion | flops 159334400 | bytes 7376000 | tf_op jit(solution)/shard_map/dtcariv,dtarjv->dtcarij/dot_general | solution.py:122
  90.2 8.0 %copy.141 = bf16[2,2,2,5,64,5,64]{6,5,2,1,0,4,3:T(8,128)(2,1)} copy(bf16[2,2,2,5,64,5,64]{4,6,2,5,3,1,0:T(8,128)(2,1)} %get-tuple-element.71) | data formatting | bytes 3276800 | tf_op jit(solution)/shard_map/reshape | solution.py:125
  98.2 7.2 %reshape.251 = bf16[2,2,2,320,320]{4,2,1,0,3:T(2,128)(2,1)S(1)} reshape(bf16[2,2,2,5,64,5,64]{6,5,2,1,0,4,3:T(8,128)(2,1)} %copy.141) | data formatting | bytes 3276800 | tf_op jit(solution)/shard_map/reshape | solution.py:125
  105.4 68.7 %all_to_all.4 = bf16[2,2,2,320,320]{4,2,1,0,3:T(2,128)(2,1)S(1)} all-to-all(bf16[2,2,2,320,320]{4,2,1,0,3:T(2,128)(2,1)S(1)} %reshape.251), channel_id=1, replica_groups=mesh['date'=32,'strip'=8] {'date'}, dimensions={3} | all-to-all | bytes 3276800 | tf_op jit(solution)/shard_map/all_to_all | solution.py:151
  174.4 3.0 %copy.132 = f32[2,2,2,320,320]{4,2,3,1,0:T(2,128)S(1)} copy(f32[2,2,2,320,320]{4,3,2,1,0:T(8,128)S(1)} %copy_convert_fusion) | data formatting | bytes 6553600 | tf_op jit(solution)/shard_map/convert_element_type | solution.py:76
  178.8 9.2 %multiply_add_fusion.2 = (f32[63,2,1,10,320]{4,2,3,1,0:T(1,128)}, f32[63,2,1,10,320]{4,2,3,1,0:T(1,128)}, f32[63,2,1,10,320]{4,2,3,1,0:T(1,128)}, f32[63,2,1,10,320]{4,2,3,1,0:T(1,128)S(1)}) fusion(f32[64,2,2,10,320]{4,2,3,1,0:T(2,128)S(1)} %bitcast.214), kind=kLoop, calls=%fused_computation.35 | loop fusion | flops 4838400 | bytes 12902400 | tf_op jit(solution)/shard_map/add | solution.py:83
  187.9 7.4 %copy.134 = f32[63,2,1,10,320]{0,1,4,3,2:T(2,128)} copy(f32[63,2,1,10,320]{4,2,3,1,0:T(1,128)} %get-tuple-element.14) | data formatting | bytes 3225600 | tf_op jit(solution)/shard_map/add | solution.py:83
  195.4 7.5 %copy.135 = f32[63,2,1,10,320]{0,1,4,3,2:T(2,128)} copy(f32[63,2,1,10,320]{4,2,3,1,0:T(1,128)} %get-tuple-element.15) | data formatting | bytes 3225600 | tf_op jit(solution)/shard_map/add | solution.py:85
  202.8 3.3 %reduce_sum.128 = f32[63,2,2,16]{0,1,3,2:T(2,128)S(1)} reduce(f32[63,2,2,5,16,20]{0,1,5,4,3,2:T(2,128)} %bitcast.218, f32[]{:T(128)} %constant.100.clone.1), dimensions={3,5}, to_apply=%region_8.10 | reduce | flops 399168 | bytes 1628932 | tf_op jit(solution)/shard_map/reduce_sum | solution.py:93
  206.1 3.3 %reduce_sum.129 = f32[63,2,2,16]{0,1,3,2:T(2,128)S(1)} reduce(f32[63,2,2,5,16,20]{0,1,5,4,3,2:T(2,128)} %bitcast.219, f32[]{:T(128)} %constant.100.clone.1), dimensions={3,5}, to_apply=%region_9.11 | reduce | flops 399168 | bytes 1628932 | tf_op jit(solution)/shard_map/reduce_sum | solution.py:93
  209.4 7.4 %copy.136 = f32[63,2,1,10,320]{0,1,4,3,2:T(2,128)} copy(f32[63,2,1,10,320]{4,2,3,1,0:T(1,128)} %get-tuple-element.16) | data formatting | bytes 3225600 | tf_op jit(solution)/shard_map/add | solution.py:86
  216.8 3.2 %reduce_sum.130 = f32[63,2,2,16]{0,1,3,2:T(2,128)S(1)} reduce(f32[63,2,2,5,16,20]{0,1,5,4,3,2:T(2,128)} %bitcast.221, f32[]{:T(128)} %constant.100.clone.1), dimensions={3,5}, to_apply=%region_10.12 | reduce | flops 399168 | bytes 1628932 | tf_op jit(solution)/shard_map/reduce_sum | solution.py:93
  220.1 4.9 %copy.137 = f32[63,2,1,10,320]{0,1,4,3,2:T(2,128)} copy(f32[63,2,1,10,320]{4,2,3,1,0:T(1,128)S(1)} %get-tuple-element.17) | data formatting | bytes 3225600 | tf_op jit(solution)/shard_map/sub | solution.py:84
  225.0 3.3 %reduce_sum.131 = f32[63,2,2,16]{0,1,3,2:T(2,128)S(1)} reduce(f32[63,2,2,5,16,20]{0,1,5,4,3,2:T(2,128)} %bitcast.220, f32[]{:T(128)} %constant.100.clone.1), dimensions={3,5}, to_apply=%region_11.13 | reduce | flops 399168 | bytes 1628932 | tf_op jit(solution)/shard_map/reduce_sum | solution.py:93
  229.0 8.8 %reduce_sum.118 = bf16[2,320,320]{2,1,0:T(8,128)(2,1)S(1)} reduce(bf16[32,2,320,320]{3,2,1,0:T(8,128)(2,1)} %bitcast.215, bf16[]{:T(256)} %constant.94.clone.1), dimensions={0}, to_apply=%region_0.1 | reduce | flops 6348800 | bytes 13516802 | tf_op jit(solution)/shard_map/reduce_sum | solution.py:31
  237.8 4.0 %all-gather.7.cloned.1.call-done = bf16[64,320,320]{2,1,0:T(8,128)(2,1)} async-done(((bf16[2,320,320]{2,1,0:T(8,128)(2,1)}), bf16[64,320,320]{2,1,0:T(8,128)(2,1)}) %all-gather.7.cloned.1.call-update) | async-done | bytes 13107216 | tf_op jit(solution)/shard_map/all_gather | solution.py:31
  241.8 8.6 %reduce_sum.119 = bf16[2,320,320]{2,1,0:T(8,128)(2,1)S(1)} reduce(bf16[32,2,320,320]{3,2,1,0:T(8,128)(2,1)} %bitcast.216, bf16[]{:T(256)} %constant.94.clone.1), dimensions={0}, to_apply=%region_1.2 | reduce | flops 6348800 | bytes 13516802 | tf_op jit(solution)/shard_map/reduce_sum | solution.py:31
  257.7 2.9 %copy.124 = f32[2,5,64,5,64]{2,4,3,1,0:T(8,128)} copy(f32[2,5,64,5,64]{4,3,2,1,0:T(8,128)} %get-tuple-element.13) | data formatting | bytes 1638400 | tf_op jit(solution)/shard_map/mul | solution.py:67
  260.6 4.4 %add_reduce_fusion.1 = (f32[2,2,5,5]{3,2,1,0:T(8,128)S(1)}, f32[2,2,5,5]{3,2,1,0:T(8,128)S(1)}, f32[2,2,5,5]{3,2,1,0:T(8,128)S(1)}) fusion(f32[2,2,2,5,64,5,64]{4,6,2,5,3,1,0:T(8,128)} %get-tuple-element.70, f32[2,5,64,5,64]{2,4,3,1,0:T(8,128)} %copy.124, f32[2,5,64,5,64]{2,4,3,1,0:T(8,128)S(1)} %copy.103), kind=kLoop, calls=%fused_computation.6 | loop fusion | flops 4914900 | bytes 4916400 | tf_op jit(solution)/shard_map/reduce_sum | solution.py:67
  (90 shorter events, 41.1 us)
Async XLA Ops:
  7.2 221.8 %all-gather.5.cloned.1.call-start = ((), (), s32[]{:S(2)}) async-start(), calls=%async_computation.1 | async-start | bytes 16220160 | tf_op jit(solution)/shard_map/all_gather | solution.py:31
  13.2 8.9 %copy-start = (bf16[2,2,2,344,320]{3,4,2,1,0:T(8,128)(2,1)S(1)}, bf16[2,2,2,344,320]{3,4,2,1,0:T(8,128)(2,1)}, u32[]{:S(2)}) copy-start(bf16[2,2,2,344,320]{3,4,2,1,0:T(8,128)(2,1)} %param.5) | copy-start | bytes 5283844
  15.2 14.6 %copy-start.1 = (s32[2,2,2,5,5]{4,2,3,1,0:T(2,128)S(1)}, s32[2,2,2,5,5]{4,2,3,1,0:T(2,128)}, u32[]{:S(2)}) copy-start(s32[2,2,2,5,5]{4,2,3,1,0:T(2,128)} %param.6) | copy-start | bytes 2404
  15.2 14.6 %copy-start.2 = (s32[2,2,2,5,5]{4,2,3,1,0:T(2,128)S(1)}, s32[2,2,2,5,5]{4,2,3,1,0:T(2,128)}, u32[]{:S(2)}) copy-start(s32[2,2,2,5,5]{4,2,3,1,0:T(2,128)} %param.7) | copy-start | bytes 2404
  18.2 223.6 %all-gather.7.cloned.1.call-start = ((), (), s32[]{:S(2)}) async-start(), calls=%async_computation.2 | async-start | bytes 16220160 | tf_op jit(solution)/shard_map/all_gather | solution.py:31
  22.2 14.7 %collective-permute-start.1 = (bf16[2,2,2,344,12]{3,4,2,1,0:T(8,128)(2,1)S(1)}, bf16[2,2,2,344,12]{3,4,2,1,0:T(8,128)(2,1)S(1)}, u32[]{:S(2)}, u32[]{:S(2)}) collective-permute-start(bf16[2,2,2,344,12]{3,4,2,1,0:T(8,128)(2,1)S(1)} %get-tuple-element.20), channel_id=1, source_target_pairs={{1,0},{2,1},{3,2},{4,3},{5,4},{6,5},{7,6},{9,8},{10,9},{11,10},{12... | collective-permute-start | bytes 198152 | tf_op jit(solution)/shard_map/ppermute | solution.py:24
  23.5 13.5 %collective-permute-start = (bf16[2,2,2,344,12]{3,4,2,1,0:T(8,128)(2,1)S(1)}, bf16[2,2,2,344,12]{3,4,2,1,0:T(8,128)(2,1)S(1)}, u32[]{:S(2)}, u32[]{:S(2)}) collective-permute-start(bf16[2,2,2,344,12]{3,4,2,1,0:T(8,128)(2,1)S(1)} %get-tuple-element.21), channel_id=1, source_target_pairs={{0,1},{1,2},{2,3},{3,4},{4,5},{5,6},{6,7},{8,9},{9,10},{10,11},{11... | collective-permute-start | bytes 198152 | tf_op jit(solution)/shard_map/ppermute | solution.py:21
Sparse Core Ops, SparseCore 0:
  18.3 98.7 all-gather.4
  118.9 122.8 all-gather.6
